TPU v7x, 256 devices: a whole 4x4x8 slice. The times are simulated.
256 devices in a mesh: group: 16 (over z, core), blk: 16 (over y, x).
Axes of the slice: x: 4, y: 4, z: 8, core: 2. Of those that a mesh axis runs over, the one named last changes fastest.
Arguments:
- hamiltonian: bfloat16 [4096, 18, 64, 256], P(('group', 'blk')), may hold values from -0.09375 to 0.09375
- block_columns: int32 [4096, 18, 4], P(('group', 'blk')), may hold values from 0 to 15, as said below
- potential: float32 [262144], P(('group', 'blk')), may hold values from -1 to 1
- trial_slab: float32 [262144, 128], P(('group', 'blk')), may hold values from -40 to 40
Outputs:
- ortho_slab: float32 [262144, 128], P(('group', 'blk'))
- upper_factor: float32 [128, 128], replicated
Inputs may be any that keep to these rules, and one draw needn't show every extreme that they name: `block_columns`: for each row block and each source, the 4 entries are distinct.
All inputs are finite; a program needn't handle non-finite values.
Results may differ from a plain program's by a relative error of at most 0.0021.
Values may be sent and summed in bfloat16 or wider, within the bound.
A program may use at most 64 MiB of HBM per device.

v0:
```python
import jax
import jax.numpy as jnp
from jax import lax
from jax.sharding import PartitionSpec as P

precise = lax.Precision.HIGHEST


def neighbours(block):
    count = lax.axis_size("group")
    forward = [(i, i + 1) for i in range(count - 1)]
    backward = [(i + 1, i) for i in range(count - 1)]
    below = lax.ppermute(block, "group", forward)
    above = lax.ppermute(block, "group", backward)
    return (below, above)


def couple_all(hamiltonian, block_columns, rounded):
    shard_blocks, nsrc, block_size, width = hamiltonian.shape
    per_source = block_columns.shape[2]
    states = rounded.shape[2]
    gathered = lax.all_gather(rounded, "blk", axis=0, tiled=True)
    below, above = neighbours(rounded)
    table = jnp.concatenate([gathered, below, above], axis=0)
    offsets = (jnp.arange(nsrc, dtype=jnp.int32) * shard_blocks)[None, :, None]
    index = block_columns + offsets
    picked = table[index.reshape(-1)].reshape(shard_blocks, nsrc, per_source * block_size, states)
    return jnp.einsum("rsik,rskn->rin", hamiltonian, picked, preferred_element_type=jnp.float32)


def on_device(hamiltonian, block_columns, potential, trial_slab):
    shard_blocks = hamiltonian.shape[0]
    block_size = hamiltonian.shape[2]
    states = trial_slab.shape[1]
    start_slab = trial_slab.reshape(shard_blocks, block_size, states)
    weights = potential.reshape(shard_blocks, block_size, 1)
    coupled_start = couple_all(hamiltonian, block_columns, start_slab.astype(jnp.bfloat16))
    filtered_once = 0.5 * (coupled_start + weights * start_slab)
    coupled_next = couple_all(hamiltonian, block_columns, filtered_once.astype(jnp.bfloat16))
    filtered = coupled_next + weights * filtered_once - start_slab
    flat = filtered.reshape(shard_blocks * block_size, states)
    rows_total = flat.shape[0] * lax.axis_size("group") * lax.axis_size("blk")
    local_gram = jnp.dot(flat.T, flat, precision=precise)
    gram = lax.psum(local_gram, ("group", "blk")) / rows_total
    lower = jnp.linalg.cholesky(gram)
    ortho_slab = lax.linalg.triangular_solve(
        lower, flat, left_side=False, lower=True, transpose_a=True
    )
    return (ortho_slab, jnp.transpose(lower))


def solution(mesh):
    placed = (
        P(("group", "blk"), None, None, None),
        P(("group", "blk"), None, None),
        P(("group", "blk")),
        P(("group", "blk"), None),
    )
    return jax.shard_map(
        on_device,
        mesh=mesh,
        in_specs=placed,
        out_specs=(P(("group", "blk"), None), P()),
        check_vma=False,
    )
```

profile of v0, /device:TPU:1, one launch (start us, length us, event | category | flops | bytes accessed | tf_op | source)
XLA Modules:
  0.0 493.7 jit_solution(8105677238921476546)
XLA Ops:
  7.2 0.0 all-gather.3.cloned.1.call-start
  7.2 1.8 convert_element_type.6
  9.0 0.0 all-gather.3.cloned.1.call-update
  9.0 0.0 all-gather.5.cloned.1.call-start
  9.1 5.1 %collective-permute-start.1 = (bf16[16,64,128]{2,1,0:T(8,128)(2,1)}, bf16[16,64,128]{2,1,0:T(8,128)(2,1)S(1)}, u32[]{:S(2)}, u32[]{:S(2)}) collective-permute-start(bf16[16,64,128]{2,1,0:T(8,128)(2,1)} %convert_element_type.6), channel_id=1, source_target_pairs={{16,0},{32,16},{48,32},{64,48},{80,64},{96,80},{112,96},{128,112},... | collective-permute-start | bytes 786440 | tf_op jit(solution)/shard_map/ppermute | solution.py:14
  14.2 1.9 collective-permute-start
  16.2 0.8 broadcast_add_fusion
  16.9 0.8 mul.37
  17.7 0.2 copy.13
  17.9 0.1 reshape.64
  18.1 0.2 collective-permute-done.1
  18.3 1.5 collective-permute-done
  19.8 51.6 %all-gather.3.cloned.1.call-done = bf16[256,64,128]{2,1,0:T(8,128)(2,1)} async-done(((bf16[16,64,128]{2,1,0:T(8,128)(2,1)}), bf16[256,64,128]{2,1,0:T(8,128)(2,1)}) %all-gather.3.cloned.1.call-update) | async-done | bytes 4194320 | tf_op jit(solution)/shard_map/all_gather | solution.py:22
  71.4 4.2 pad_maximum_fusion
  75.5 0.0 copy-start
  75.5 29.1 %gather_fusion = bf16[1152,64,128]{2,1,0:T(8,128)(2,1)} fusion(bf16[288,64,128]{2,1,0:T(8,128)(2,1)} %pad_maximum_fusion, s32[2048]{0:T(1024)S(1)} %pad_clamp_fusion), kind=kCustom, calls=%fused_computation | custom fusion | bytes 37753344 | tf_op jit(solution)/shard_map/gather | solution.py:27
  104.6 0.0 copy-done
  104.6 13.5 %multiply_convert_fusion = (bf16[16,64,128]{2,1,0:T(8,128)(2,1)}, f32[16,64,128]{2,1,0:T(8,128)S(1)}) fusion(f32[16,64,128]{2,1,0:T(8,128)S(1)} %bitcast.44, f32[16,64]{1,0:T(8,128)S(1)} %mul.37, bf16[16,18,64,256]{3,2,1,0:T(8,128)(2,1)} %param.4, bf16[16,18,256,128]{3,2,1,0:T(8,128)(2,1)} %bitcast.41), kind=kOutput, calls=%fused_computation.10 | convolution fusion | flops 1208483840 | bytes 29626368 | tf_op jit(solution)/shard_map/rsik,rskn->rin/dot_general | solution.py:28
  118.2 0.0 all-gather.5.cloned.1.call-update
  118.2 0.0 all-reduce.2.cloned.1.call-start
  118.2 2.6 collective-permute-start.3
  120.8 3.3 collective-permute-start.2
  124.1 2.1 collective-permute-done.3
  126.2 1.3 collective-permute-done.2
  127.5 47.1 %all-gather.5.cloned.1.call-done = bf16[256,64,128]{2,1,0:T(8,128)(2,1)} async-done(((bf16[16,64,128]{2,1,0:T(8,128)(2,1)}), bf16[256,64,128]{2,1,0:T(8,128)(2,1)}) %all-gather.5.cloned.1.call-update) | async-done | bytes 4194320 | tf_op jit(solution)/shard_map/all_gather | solution.py:22
  174.6 4.2 pad_maximum_fusion.1
  178.8 29.2 %gather_fusion.1 = bf16[1152,64,128]{2,1,0:T(8,128)(2,1)} fusion(bf16[288,64,128]{2,1,0:T(8,128)(2,1)} %pad_maximum_fusion.1, s32[2048]{0:T(1024)S(1)} %pad_clamp_fusion), kind=kCustom, calls=%fused_computation.1 | custom fusion | bytes 37753344 | tf_op jit(solution)/shard_map/gather | solution.py:27
  208.0 12.8 %fusion.2 = f32[16,64,128]{2,1,0:T(8,128)S(1)} fusion(f32[16,64,128]{2,1,0:T(8,128)S(1)} %bitcast.45, bf16[16,18,64,256]{3,2,1,0:T(8,128)(2,1)} %param.4, bf16[16,18,256,128]{3,2,1,0:T(8,128)(2,1)} %bitcast.40, f32[16,64,128]{2,1,0:T(8,128)S(1)} %get-tuple-element.11, f32[16,64]{1,0:T(8,128)S(1)} %broadcast_multiply_fusion.1), kind=kOutput, calls=%fused_computation.8 | convolution fusion | flops 1208352768 | bytes 29888512 | tf_op jit(solution)/shard_map/rsik,rskn->rin/dot_general | solution.py:28
  220.8 1.6 convolution_bitcast_fusion.2
  222.5 0.0 all-reduce.2.cloned.1.call-update
  222.5 237.9 %all-reduce.2.cloned.1.call-done = f32[128,128]{0,1:T(8,128)} async-done(((f32[128,128]{0,1:T(8,128)}), f32[128,128]{0,1:T(8,128)}) %all-reduce.2.cloned.1.call-update) | async-done | bytes 65552 | tf_op jit(solution)/shard_map/psum | solution.py:44
  460.4 0.8 broadcast_multiply_fusion
  461.3 0.1 copy.15
  461.4 0.9 fusion.5
  462.2 11.7 %cholesky.16 = f32[128,128]{1,0:T(8,128)S(1)} custom-call(f32[128,128]{1,0:T(8,128)S(1)} %fusion.5), custom_call_target="Cholesky" | custom-call | tf_op jit(solution)/shard_map/jit(cholesky)/cholesky | solution.py:45
  474.0 0.6 compare_reduce_fusion
  474.6 0.7 fusion.6
  475.3 0.7 copy.16
  476.0 9.8 %custom-call.6 = f32[1,128,128]{1,2,0:T(8,128)S(1)} custom-call(f32[1,128,128]{2,1,0:T(8,128)S(1)} %get-tuple-element.9), custom_call_target="InvertDiagBlocksLowerTriangular" | custom-call | tf_op jit(solution)/shard_map/triangular_solve | solution.py:46
  485.8 1.4 fusion.3
  (5 shorter events, 0.1 us)
Async XLA Ops:
  7.2 64.2 %all-gather.3.cloned.1.call-start = ((), (), s32[]{:S(2)}) async-start(), calls=%async_computation | async-start | bytes 4456448 | tf_op jit(solution)/shard_map/all_gather | solution.py:22
  9.0 165.6 %all-gather.5.cloned.1.call-start = ((), (), s32[]{:S(2)}) async-start(), calls=%async_computation.1 | async-start | bytes 4456448 | tf_op jit(solution)/shard_map/all_gather | solution.py:22
  9.1 9.2 %collective-permute-start.1 = (bf16[16,64,128]{2,1,0:T(8,128)(2,1)}, bf16[16,64,128]{2,1,0:T(8,128)(2,1)S(1)}, u32[]{:S(2)}, u32[]{:S(2)}) collective-permute-start(bf16[16,64,128]{2,1,0:T(8,128)(2,1)} %convert_element_type.6), channel_id=1, source_target_pairs={{16,0},{32,16},{48,32},{64,48},{80,64},{96,80},{112,96},{128,112},... | collective-permute-start | bytes 786440 | tf_op jit(solution)/shard_map/ppermute | solution.py:14
  14.2 5.5 %collective-permute-start = (bf16[16,64,128]{2,1,0:T(8,128)(2,1)}, bf16[16,64,128]{2,1,0:T(8,128)(2,1)S(1)}, u32[]{:S(2)}, u32[]{:S(2)}) collective-permute-start(bf16[16,64,128]{2,1,0:T(8,128)(2,1)} %convert_element_type.6), channel_id=1, source_target_pairs={{0,16},{16,32},{32,48},{48,64},{64,80},{80,96},{96,112},{112,128},... | collective-permute-start | bytes 786440 | tf_op jit(solution)/shard_map/ppermute | solution.py:13
  75.5 29.1 %copy-start = (f32[1024,128]{1,0:T(8,128)S(1)}, f32[1024,128]{1,0:T(8,128)}, u32[]{:S(2)}) copy-start(f32[1024,128]{1,0:T(8,128)} %param.7) | copy-start | bytes 1572868
  118.2 342.3 %all-reduce.2.cloned.1.call-start = ((), (), s32[]{:S(2)}) async-start(), calls=%async_computation.2 | async-start | bytes 131072 | tf_op jit(solution)/shard_map/psum | solution.py:44
  118.2 8.0 %collective-permute-start.3 = (bf16[16,64,128]{2,1,0:T(8,128)(2,1)}, bf16[16,64,128]{2,1,0:T(8,128)(2,1)S(1)}, u32[]{:S(2)}, u32[]{:S(2)}) collective-permute-start(bf16[16,64,128]{2,1,0:T(8,128)(2,1)} %get-tuple-element.10), channel_id=1, source_target_pairs={{16,0},{32,16},{48,32},{64,48},{80,64},{96,80},{112,96},{128,112},... | collective-permute-start | bytes 786440 | tf_op jit(solution)/shard_map/ppermute | solution.py:14
  120.8 6.7 %collective-permute-start.2 = (bf16[16,64,128]{2,1,0:T(8,128)(2,1)}, bf16[16,64,128]{2,1,0:T(8,128)(2,1)S(1)}, u32[]{:S(2)}, u32[]{:S(2)}) collective-permute-start(bf16[16,64,128]{2,1,0:T(8,128)(2,1)} %get-tuple-element.10), channel_id=1, source_target_pairs={{0,16},{16,32},{32,48},{48,64},{64,80},{80,96},{96,112},{112,128},... | collective-permute-start | bytes 786440 | tf_op jit(solution)/shard_map/ppermute | solution.py:13
Sparse Core Ops, SparseCore 0:
  11.0 60.3 all-gather.2
  118.3 56.2 all-gather.4
  222.6 237.7 all-reduce.1
where the time goes:
time: 494 us
  waiting for transfers between devices  342 us (69%)
  local copies, waits for them, and re-layouts  60.2 us (12%)
  other arithmetic  35.5 us (7%)
  matrix products  29.3 us (6%)
  between operations  13.9 us (3%)
  starting transfers between devices  13 us (3%)
    psum x1, waiting for transfers between devices, on_device(): gram = lax.psum(local_gram, ('group', 'blk')) / rows_total  238 us
    all_gather x2, waiting for transfers between devices, couple_all(): gathered = lax.all_gather(rounded, 'blk', axis=0, tiled=True)  98.7 us
    gather x2, local copies, waits for them, and re-layouts, couple_all(): table[index.reshape(-1)]  58.3 us
    dot_general x2, matrix products, couple_all(): jnp.einsum('rsik,rskn->rin', hamiltonian, picked, preferred_element_type=...  26.3 us
    another operation x3, other arithmetic, on_device(): lower = jnp.linalg.cholesky(gram)  12.4 us
  transfers between devices with their start and end apart: 7, of which 7 were waited for; matrix products, arithmetic and copies ran while one was open for 0% of the time, Pallas kernels for 0%

commit v1 on v0

--- a/solution.py
+++ b/solution.py
@@ -41,7 +41,7 @@
     flat = filtered.reshape(shard_blocks * block_size, states)
     rows_total = flat.shape[0] * lax.axis_size("group") * lax.axis_size("blk")
     local_gram = jnp.dot(flat.T, flat, precision=precise)
-    gram = lax.psum(local_gram, ("group", "blk")) / rows_total
+    gram = jnp.sum(lax.all_gather(local_gram, ("group", "blk")), axis=0) / rows_total
     lower = jnp.linalg.cholesky(gram)
     ortho_slab = lax.linalg.triangular_solve(
         lower, flat, left_side=False, lower=True, transpose_a=True

time: 494 us -> 386 us (0.78)
  waiting for transfers between devices: 342 us -> 229 us
    psum x1 -> x0, waiting for transfers between devices: 238 us -> none  [on_device(): gram = lax.psum(local_gram, ('group', 'blk')) / rows_total]
    all_gather x0 -> x1, waiting for transfers between devices: none -> 125 us  [on_device(): lax.all_gather(local_gram, ('group', 'blk'))]
    reduce_sum x0 -> x1, other arithmetic: none -> 6.59 us  [on_device(): jnp.sum(lax.all_gather(local_gram, ('group', 'blk')), axis=0) / rows_total]
where the time goes in v1:
time: 386 us
  waiting for transfers between devices  229 us (59%)
  local copies, waits for them, and re-layouts  60.2 us (16%)
  other arithmetic  40.4 us (10%)
  matrix products  29.3 us (8%)
  between operations  13.9 us (4%)
  starting transfers between devices  13 us (3%)
    all_gather x1, waiting for transfers between devices, on_device(): lax.all_gather(local_gram, ('group', 'blk'))  125 us
    all_gather x2, waiting for transfers between devices, couple_all(): gathered = lax.all_gather(rounded, 'blk', axis=0, tiled=True)  98.7 us
    gather x2, local copies, waits for them, and re-layouts, couple_all(): table[index.reshape(-1)]  58.3 us
    dot_general x2, matrix products, couple_all(): jnp.einsum('rsik,rskn->rin', hamiltonian, picked, preferred_element_type=...  26.3 us
    another operation x3, other arithmetic, on_device(): lower = jnp.linalg.cholesky(gram)  12.4 us
    another operation x1, other arithmetic, on_device(): lax.linalg.triangular_solve(lower, flat, left_side=False, lower=True, tra...  9.81 us
    concatenate x2, other arithmetic, couple_all(): table = jnp.concatenate([gathered, below, above], axis=0)  8.31 us
    ppermute x2, starting transfers between devices, neighbours(): above = lax.ppermute(block, 'group', backward)  7.74 us
  transfers between devices with their start and end apart: 7, of which 7 were waited for; matrix products, arithmetic and copies ran while one was open for 0% of the time, Pallas kernels for 0%

profile of v1, /device:TPU:1, one launch (start us, length us, event | category | flops | bytes accessed | tf_op | source)
XLA Modules:
  0.0 385.9 jit_solution(13532769947968261188)
XLA Ops:
  7.2 0.0 all-gather.5.cloned.1.call-start
  7.2 1.8 convert_element_type.6
  9.0 0.0 all-gather.5.cloned.1.call-update
  9.0 0.0 all-gather.7.cloned.1.call-start
  9.1 5.1 %collective-permute-start.1 = (bf16[16,64,128]{2,1,0:T(8,128)(2,1)}, bf16[16,64,128]{2,1,0:T(8,128)(2,1)S(1)}, u32[]{:S(2)}, u32[]{:S(2)}) collective-permute-start(bf16[16,64,128]{2,1,0:T(8,128)(2,1)} %convert_element_type.6), channel_id=1, source_target_pairs={{16,0},{32,16},{48,32},{64,48},{80,64},{96,80},{112,96},{128,112},... | collective-permute-start | bytes 786440 | tf_op jit(solution)/shard_map/ppermute | solution.py:14
  14.2 1.9 collective-permute-start
  16.2 0.8 broadcast_add_fusion
  16.9 0.8 mul.37
  17.7 0.2 copy.11
  17.9 0.1 reshape.64
  18.1 0.2 collective-permute-done.1
  18.3 1.5 collective-permute-done
  19.8 51.6 %all-gather.5.cloned.1.call-done = bf16[256,64,128]{2,1,0:T(8,128)(2,1)} async-done(((bf16[16,64,128]{2,1,0:T(8,128)(2,1)}), bf16[256,64,128]{2,1,0:T(8,128)(2,1)}) %all-gather.5.cloned.1.call-update) | async-done | bytes 4194320 | tf_op jit(solution)/shard_map/all_gather | solution.py:22
  71.4 4.2 %pad_maximum_fusion = bf16[288,64,128]{2,1,0:T(8,128)(2,1)} fusion(bf16[16,64,128]{2,1,0:T(8,128)(2,1)S(1)} %collective-permute-done.1, bf16[16,64,128]{2,1,0:T(8,128)(2,1)S(1)} %collective-permute-done, bf16[256,64,128]{2,1,0:T(8,128)(2,1)} %all-gather.5.cloned.1.call-done), kind=kLoop, calls=%fused_computation.2 | loop fusion | flops 4718592 | bytes 9437184 | tf_op jit(solution)/shard_map/concatenate | solution.py:24
  75.5 0.0 copy-start
  75.5 29.1 %gather_fusion = bf16[1152,64,128]{2,1,0:T(8,128)(2,1)} fusion(bf16[288,64,128]{2,1,0:T(8,128)(2,1)} %pad_maximum_fusion, s32[2048]{0:T(1024)S(1)} %pad_clamp_fusion), kind=kCustom, calls=%fused_computation | custom fusion | bytes 37753344 | tf_op jit(solution)/shard_map/gather | solution.py:27
  104.6 0.0 copy-done
  104.6 13.5 %multiply_convert_fusion = (bf16[16,64,128]{2,1,0:T(8,128)(2,1)}, f32[16,64,128]{2,1,0:T(8,128)S(1)}) fusion(f32[16,64,128]{2,1,0:T(8,128)S(1)} %bitcast.46, f32[16,64]{1,0:T(8,128)S(1)} %mul.37, bf16[16,18,64,256]{3,2,1,0:T(8,128)(2,1)} %param.4, bf16[16,18,256,128]{3,2,1,0:T(8,128)(2,1)} %bitcast.42), kind=kOutput, calls=%fused_computation.10 | convolution fusion | flops 1208483840 | bytes 29626368 | tf_op jit(solution)/shard_map/rsik,rskn->rin/dot_general | solution.py:28
  118.2 0.0 all-gather.7.cloned.1.call-update
  118.2 0.0 all-gather.9.cloned.1.call-start
  118.2 2.6 collective-permute-start.3
  120.8 3.3 collective-permute-start.2
  124.1 2.1 collective-permute-done.3
  126.2 1.3 collective-permute-done.2
  127.5 47.1 %all-gather.7.cloned.1.call-done = bf16[256,64,128]{2,1,0:T(8,128)(2,1)} async-done(((bf16[16,64,128]{2,1,0:T(8,128)(2,1)}), bf16[256,64,128]{2,1,0:T(8,128)(2,1)}) %all-gather.7.cloned.1.call-update) | async-done | bytes 4194320 | tf_op jit(solution)/shard_map/all_gather | solution.py:22
  174.6 4.2 %pad_maximum_fusion.1 = bf16[288,64,128]{2,1,0:T(8,128)(2,1)} fusion(bf16[16,64,128]{2,1,0:T(8,128)(2,1)S(1)} %collective-permute-done.3, bf16[16,64,128]{2,1,0:T(8,128)(2,1)S(1)} %collective-permute-done.2, bf16[256,64,128]{2,1,0:T(8,128)(2,1)} %all-gather.7.cloned.1.call-done), kind=kLoop, calls=%fused_computation.3 | loop fusion | flops 4718592 | bytes 9437184 | tf_op jit(solution)/shard_map/concatenate | solution.py:24
  178.8 29.2 %gather_fusion.1 = bf16[1152,64,128]{2,1,0:T(8,128)(2,1)} fusion(bf16[288,64,128]{2,1,0:T(8,128)(2,1)} %pad_maximum_fusion.1, s32[2048]{0:T(1024)S(1)} %pad_clamp_fusion), kind=kCustom, calls=%fused_computation.1 | custom fusion | bytes 37753344 | tf_op jit(solution)/shard_map/gather | solution.py:27
  208.0 12.8 %fusion.2 = f32[16,64,128]{2,1,0:T(8,128)S(1)} fusion(f32[16,64,128]{2,1,0:T(8,128)S(1)} %bitcast.47, bf16[16,18,64,256]{3,2,1,0:T(8,128)(2,1)} %param.4, bf16[16,18,256,128]{3,2,1,0:T(8,128)(2,1)} %bitcast.41, f32[16,64,128]{2,1,0:T(8,128)S(1)} %get-tuple-element.11, f32[16,64]{1,0:T(8,128)S(1)} %broadcast_multiply_fusion), kind=kOutput, calls=%fused_computation.8 | convolution fusion | flops 1208352768 | bytes 29888512 | tf_op jit(solution)/shard_map/rsik,rskn->rin/dot_general | solution.py:28
  220.8 1.6 convolution_bitcast_fusion.2
  222.5 0.0 all-gather.9.cloned.1.call-update
  222.5 125.2 %all-gather.9.cloned.1.call-done = f32[32768,128]{1,0:T(8,128)} async-done(((f32[128,128]{1,0:T(8,128)}), f32[32768,128]{1,0:T(8,128)}) %all-gather.9.cloned.1.call-update) | async-done | bytes 16777232 | tf_op jit(solution)/shard_map/all_gather | solution.py:44
  347.7 6.6 %reduce_sum.11 = f32[128,128]{1,0:T(8,128)S(1)} reduce(f32[256,128,128]{2,1,0:T(8,128)} %bitcast.43, f32[]{:T(128)} %constant.49.clone.1), dimensions={0}, to_apply=%region_0.0 | reduce | flops 4177920 | bytes 16842756 | tf_op jit(solution)/shard_map/reduce_sum | solution.py:44
  354.3 0.1 copy.12
  354.4 11.7 %cholesky.16 = f32[128,128]{1,0:T(8,128)S(1)} custom-call(f32[128,128]{1,0:T(8,128)S(1)} %fusion.5), custom_call_target="Cholesky" | custom-call | tf_op jit(solution)/shard_map/jit(cholesky)/cholesky | solution.py:45
  366.1 0.6 compare_reduce_fusion
  366.8 0.7 fusion.6
  367.4 0.7 copy.13
  368.2 9.8 %custom-call.6 = f32[1,128,128]{1,2,0:T(8,128)S(1)} custom-call(f32[1,128,128]{2,1,0:T(8,128)S(1)} %get-tuple-element.9), custom_call_target="InvertDiagBlocksLowerTriangular" | custom-call | tf_op jit(solution)/shard_map/triangular_solve | solution.py:46
  378.0 1.4 fusion.3
  (6 shorter events, 0.1 us)
Async XLA Ops:
  7.2 64.2 %all-gather.5.cloned.1.call-start = ((), (), s32[]{:S(2)}) async-start(), calls=%async_computation | async-start | bytes 4456448 | tf_op jit(solution)/shard_map/all_gather | solution.py:22
  9.0 165.6 %all-gather.7.cloned.1.call-start = ((), (), s32[]{:S(2)}) async-start(), calls=%async_computation.1 | async-start | bytes 4456448 | tf_op jit(solution)/shard_map/all_gather | solution.py:22
  9.1 9.2 %collective-permute-start.1 = (bf16[16,64,128]{2,1,0:T(8,128)(2,1)}, bf16[16,64,128]{2,1,0:T(8,128)(2,1)S(1)}, u32[]{:S(2)}, u32[]{:S(2)}) collective-permute-start(bf16[16,64,128]{2,1,0:T(8,128)(2,1)} %convert_element_type.6), channel_id=1, source_target_pairs={{16,0},{32,16},{48,32},{64,48},{80,64},{96,80},{112,96},{128,112},... | collective-permute-start | bytes 786440 | tf_op jit(solution)/shard_map/ppermute | solution.py:14
  14.2 5.5 %collective-permute-start = (bf16[16,64,128]{2,1,0:T(8,128)(2,1)}, bf16[16,64,128]{2,1,0:T(8,128)(2,1)S(1)}, u32[]{:S(2)}, u32[]{:S(2)}) collective-permute-start(bf16[16,64,128]{2,1,0:T(8,128)(2,1)} %convert_element_type.6), channel_id=1, source_target_pairs={{0,16},{16,32},{32,48},{48,64},{64,80},{80,96},{96,112},{112,128},... | collective-permute-start | bytes 786440 | tf_op jit(solution)/shard_map/ppermute | solution.py:13
  75.5 29.1 %copy-start = (f32[1024,128]{1,0:T(8,128)S(1)}, f32[1024,128]{1,0:T(8,128)}, u32[]{:S(2)}) copy-start(f32[1024,128]{1,0:T(8,128)} %param.7) | copy-start | bytes 1572868
  118.2 229.5 %all-gather.9.cloned.1.call-start = ((), (), s32[]{:S(2)}) async-start(), calls=%async_computation.2 | async-start | bytes 16842752 | tf_op jit(solution)/shard_map/all_gather | solution.py:44
  118.2 8.0 %collective-permute-start.3 = (bf16[16,64,128]{2,1,0:T(8,128)(2,1)}, bf16[16,64,128]{2,1,0:T(8,128)(2,1)S(1)}, u32[]{:S(2)}, u32[]{:S(2)}) collective-permute-start(bf16[16,64,128]{2,1,0:T(8,128)(2,1)} %get-tuple-element.10), channel_id=1, source_target_pairs={{16,0},{32,16},{48,32},{64,48},{80,64},{96,80},{112,96},{128,112},... | collective-permute-start | bytes 786440 | tf_op jit(solution)/shard_map/ppermute | solution.py:14
  120.8 6.7 %collective-permute-start.2 = (bf16[16,64,128]{2,1,0:T(8,128)(2,1)}, bf16[16,64,128]{2,1,0:T(8,128)(2,1)S(1)}, u32[]{:S(2)}, u32[]{:S(2)}) collective-permute-start(bf16[16,64,128]{2,1,0:T(8,128)(2,1)} %get-tuple-element.10), channel_id=1, source_target_pairs={{0,16},{16,32},{32,48},{48,64},{64,80},{80,96},{96,112},{112,128},... | collective-permute-start | bytes 786440 | tf_op jit(solution)/shard_map/ppermute | solution.py:13
Sparse Core Ops, SparseCore 0:
  11.0 60.3 all-gather.4
  118.3 56.2 all-gather.6
  222.6 125.0 all-gather.8
